TPU v7x, 32 devices: a whole 2x2x4 slice. The times are simulated.
32 devices in a mesh: fft: 16 (over z, y, x), grp: 2 (over core).
Axes of the slice: x: 2, y: 2, z: 4, core: 2. Of those that a mesh axis runs over, the one named last changes fastest.
Arguments:
- potential: float32 [4, 256, 256, 256], P(None, 'fft', 'grp'), may hold values from -6 to 6
- stick_mill: int32 [2, 256], replicated, may hold values from -128 to 127, as said below
- positions: int32 [3, 256], P(None, 'grp'), may hold values from 0 to 255
- aug_charge: bfloat16 [171, 256, 256], P(None, 'fft'), may hold values from -0.0234375 to 0.0234375
Outputs:
- vg_sticks: float32 [4, 2, 256, 256], P(None, None, 'fft')
- d_matrix: float32 [4, 171, 256], P(None, None, 'grp')
Inputs may be any that keep to these rules, and one draw needn't show every extreme that they name: `stick_mill`: stick k is owned by fft index k // 16; no two sticks have the same (gx, gy), and every stick has gx^2 + gy^2 < 128^2.
All inputs are finite; a program needn't handle non-finite values.
Results may differ from a plain program's by a relative error of at most 0.0029.
Values sent between devices are 32-bit elements; how exact they have to be, the bound alone decides.
A program may use at most 128 MiB of HBM per device.

v0:
```python
import functools
import math

import jax
import jax.numpy as jnp
from jax import lax
from jax.experimental import pallas as pl
from jax.experimental.pallas import tpu as pltpu
from jax.sharding import PartitionSpec as P

MESH = pl.DeviceIdType.MESH
F32 = jnp.float32
BF16 = jnp.bfloat16


def cos_sin(k, n):
    quarter = n // 4
    moved = k + n // 8
    m = jnp.bitwise_and(moved, quarter - 1) - n // 8
    q = jnp.bitwise_and(jnp.right_shift(moved, quarter.bit_length() - 1), 3)
    a = m.astype(F32) * (2.0 * math.pi / n)
    b = a * a
    s = a * (1.0 + b * (-1.0 / 6 + b * (1.0 / 120 + b * (-1.0 / 5040 + b * (1.0 / 362880)))))
    c = 1.0 + b * (-0.5 + b * (1.0 / 24 + b * (-1.0 / 720 + b * (1.0 / 40320))))
    odd = jnp.bitwise_and(q, 1) == 1
    cc = jnp.where(odd, s, c)
    ss = jnp.where(odd, c, s)
    cc = jnp.where((q == 1) | (q == 2), -cc, cc)
    ss = jnp.where(q >= 2, -ss, ss)
    return cc, ss


def split(v):
    hi = v.astype(BF16)
    lo = (v - hi.astype(F32)).astype(BF16)
    return hi, lo


def stack_table(table):
    hi, lo = split(table)
    return jnp.concatenate([hi, lo, hi], axis=0)


def stack_data(data):
    hi, lo = split(data)
    return jnp.concatenate([hi, hi, lo], axis=1)


def kernel(dims, pot_hbm, mill_ref, mill_smem, pos_ref, aug_hbm, vg_ref, d_ref,
           pot, aug, augf, qall, tx, ty, tz, part, send, recv, phase, kpos, xmid, mixed, dpart, dbuf, dsum,
           pot_sem, aug_sem, s1, r1, own_sem, s2, r2, s3, r3):
    C, ZL, YL, N, S, F, G, SL, PAIRS, ATOMS, ZC, ROWS, PER = dims
    H = ZL // ZC
    ND = F * G
    my_f = lax.axis_index("fft")
    my_g = lax.axis_index("grp")
    me = my_f * G + my_g

    def pot_copy(h, c):
        return pltpu.make_async_copy(
            pot_hbm.at[c, pl.ds(h * ZC, ZC)], pot.at[h, c], pot_sem.at[h, c])

    for h in range(H):
        for c in range(C):
            pot_copy(h, c).start()
    aug_copy = pltpu.make_async_copy(aug_hbm, aug, aug_sem)
    aug_copy.start()

    barrier = pltpu.get_barrier_semaphore()

    def greet(k, _):
        peer = lax.rem(me + k, ND)
        pl.semaphore_signal(barrier, inc=1, device_id={"fft": peer // G, "grp": lax.rem(peer, G)},
                            device_id_type=MESH)
        return 0

    lax.fori_loop(1, ND, greet, 0)

    gx = mill_ref[0:1, :]
    gy = mill_ref[1:2, :]
    cx, sx = cos_sin(lax.broadcasted_iota(jnp.int32, (N, S), 0) * gx, N)
    tx[:, :S] = stack_table(cx)
    tx[:, S:] = stack_table(sx)
    cy, sy = cos_sin((lax.broadcasted_iota(jnp.int32, (YL, S), 0) + my_g * YL) * gy, N)
    ty[0] = cy
    ty[1] = sy

    pl.semaphore_wait(barrier, ND - 1)

    def block_send(h, k):
        peer = lax.rem(me + k, ND)
        pf, pg = peer // G, lax.rem(peer, G)
        return pltpu.make_async_remote_copy(
            src_ref=send.at[h, pf], dst_ref=recv.at[my_g, my_f, h],
            send_sem=s1.at[h, pf * G + pg], recv_sem=r1.at[h, me],
            device_id={"fft": pf, "grp": pg}, device_id_type=MESH)

    def block_recv(h, k):
        peer = lax.rem(me + k, ND)
        pf, pg = peer // G, lax.rem(peer, G)
        return pltpu.make_async_remote_copy(
            src_ref=send.at[h, pf], dst_ref=recv.at[pg, pf, h],
            send_sem=s1.at[h, pf * G + pg], recv_sem=r1.at[h, peer],
            device_id={"fft": pf, "grp": pg}, device_id_type=MESH)

    def group(h, _):
        def component(c, _):
            pot_copy(h, c).wait()
            data = pot[h, c].reshape(ZC * YL, N)
            xmid[...] = jnp.dot(stack_data(data), tx[...], preferred_element_type=F32)
            re_rows = []
            im_rows = []
            for z in range(ZC):
                a = xmid[z * YL:(z + 1) * YL, :S]
                b = xmid[z * YL:(z + 1) * YL, S:]
                re_rows.append(jnp.sum(a * ty[0] - b * ty[1], axis=0, keepdims=True))
                im_rows.append(-jnp.sum(a * ty[1] + b * ty[0], axis=0, keepdims=True))
            part[0, c] = jnp.concatenate(re_rows, axis=0)
            part[1, c] = jnp.concatenate(im_rows, axis=0)
            return 0

        lax.fori_loop(0, C, component, 0)
        for f in range(F):
            pieces = [part[ri, c, :, f * SL:(f + 1) * SL] for ri in range(2) for c in range(C)]
            send[h, f] = jnp.concatenate(pieces, axis=1)

        def start(k, _):
            block_send(h, k).start()
            return 0

        lax.fori_loop(1, ND, start, 0)
        pltpu.make_async_copy(send.at[h, my_f], recv.at[my_g, my_f, h], own_sem.at[h]).start()
        return 0

    lax.fori_loop(0, H, group, 0)

    row = lax.broadcasted_iota(jnp.int32, (N, N), 0)
    col = lax.broadcasted_iota(jnp.int32, (N, N), 1) - N // 2
    cz, sz = cos_sin(row * col, N)
    tz[:, :N] = stack_table(cz)
    tz[:, N:] = stack_table(sz)
    shifted = lax.broadcasted_iota(jnp.int32, (ATOMS, N), 1) - N // 2

    def spread(r):
        rows = jnp.broadcast_to(pos_ref[r:r + 1, :].astype(F32), (ATOMS, ATOMS))
        column = jnp.transpose(rows)[:, 0:1]
        return jnp.broadcast_to(column, (ATOMS, N)).astype(jnp.int32)

    kpos[0] = spread(0)
    kpos[1] = spread(1)
    kpos[2] = spread(2) * shifted

    def phases(s, _):
        gxs = mill_smem[0, my_f * SL + s]
        gys = mill_smem[1, my_f * SL + s]
        cosine, sine = cos_sin(kpos[0] * gxs + kpos[1] * gys + kpos[2], N)
        phase[0, s] = cosine
        phase[1, s] = sine
        return 0

    lax.fori_loop(0, SL, phases, 0)

    aug_copy.wait()
    flat = aug[...].reshape(PAIRS * SL, N)
    for w in range(N // 128):
        augf[w, :PAIRS * SL, :] = flat[:, w * 128:(w + 1) * 128].astype(F32)
        augf[w, PAIRS * SL:, :] = jnp.zeros((ROWS * PER * SL - PAIRS * SL, 128), F32)
    for s in range(SL):
        for w in range(N // 128):
            picked = augf[w, pl.ds(s, ROWS * PER, stride=SL), :]
            qall[:, s * N + w * 128:s * N + (w + 1) * 128] = picked.astype(BF16)

    for h in range(H):
        pltpu.make_async_copy(send.at[h, my_f], recv.at[my_g, my_f, h], own_sem.at[h]).wait()

        def arrive(k, _):
            block_recv(h, k).wait_recv()
            return 0

        lax.fori_loop(1, ND, arrive, 0)

    gathered = recv[0]
    for g in range(1, G):
        gathered = gathered + recv[g]
    lanes = 2 * C * SL
    turned = jnp.transpose(gathered.reshape(F * ZL, lanes))
    pq = jnp.dot(stack_data(turned), tz[...], preferred_element_type=F32)
    half = C * SL
    norm = float(N) ** -1.5
    re = (pq[:half, :N] + pq[half:, N:]) * norm
    im = (pq[half:, :N] - pq[:half, N:]) * norm
    for c in range(C):
        vg_ref[c, 0] = re[c * SL:(c + 1) * SL]
        vg_ref[c, 1] = im[c * SL:(c + 1) * SL]

    my_c, my_j = my_f // PER, lax.rem(my_f, PER)

    def d_send(ci, j):
        owner = ci * PER + j
        return pltpu.make_async_remote_copy(
            src_ref=dpart.at[ci, j], dst_ref=dbuf.at[my_f],
            send_sem=s2.at[owner], recv_sem=r2.at[my_f],
            device_id={"fft": owner}, device_id_type=MESH)

    def contract(i, _):
        ci = lax.rem(my_c + 1 + i, C)
        for s in range(SL):
            vr = vg_ref[ci, 0, s:s + 1, :]
            vi = vg_ref[ci, 1, s:s + 1, :]
            mixed[:, s * N:(s + 1) * N] = (vr * phase[0, s] - vi * phase[1, s]).astype(BF16)
        out = lax.dot_general(qall[...], mixed[...], (((1,), (1,)), ((), ())), preferred_element_type=F32)
        for j in range(PER):
            dpart[ci, j] = out[j * ROWS:(j + 1) * ROWS]
        for j in range(PER):
            @pl.when(ci * PER + j != my_f)
            def _():
                d_send(ci, j).start()
        return 0

    lax.fori_loop(0, C, contract, 0)

    dbuf[my_f] = dpart[my_c, my_j]

    def d_wait(k, _):
        peer = lax.rem(my_f + k, F)
        pltpu.make_async_remote_copy(
            src_ref=dpart.at[peer // PER, lax.rem(peer, PER)], dst_ref=dbuf.at[peer],
            send_sem=s2.at[peer], recv_sem=r2.at[peer],
            device_id={"fft": peer}, device_id_type=MESH).wait_recv()
        return 0

    lax.fori_loop(1, F, d_wait, 0)
    total = dbuf[0]
    for f in range(1, F):
        total = total + dbuf[f]
    dsum[...] = total

    def out_copy(k):
        peer = lax.rem(my_f + k, F)
        return pltpu.make_async_remote_copy(
            src_ref=dsum, dst_ref=d_ref.at[my_c, my_j],
            send_sem=s3.at[peer], recv_sem=r3.at[my_f],
            device_id={"fft": peer}, device_id_type=MESH)

    def out_start(k, _):
        out_copy(k).start()
        return 0

    lax.fori_loop(1, F, out_start, 0)
    d_ref[my_c, my_j] = total

    def drain(k, _):
        for h in range(H):
            block_send(h, k).wait_send()
        return 0

    lax.fori_loop(1, ND, drain, 0)

    def finish(k, _):
        peer = lax.rem(my_f + k, F)
        pf, pj = peer // PER, lax.rem(peer, PER)
        d_send(pf, pj).wait_send()
        out_copy(k).wait_send()
        pltpu.make_async_remote_copy(
            src_ref=dsum, dst_ref=d_ref.at[pf, pj],
            send_sem=s3.at[peer], recv_sem=r3.at[peer],
            device_id={"fft": peer}, device_id_type=MESH).wait_recv()
        return 0

    lax.fori_loop(1, F, finish, 0)


def body(potential, stick_mill, positions, aug_charge):
    C, ZL, YL, N = potential.shape
    S = stick_mill.shape[1]
    F, G = lax.axis_size("fft"), lax.axis_size("grp")
    SL = S // F
    PAIRS = aug_charge.shape[0]
    ATOMS = positions.shape[1]
    ZC = min(8, ZL)
    H = ZL // ZC
    PER = F // C
    ROWS = -(-PAIRS // (PER * 8)) * 8
    ND = F * G
    dims = (C, ZL, YL, N, S, F, G, SL, PAIRS, ATOMS, ZC, ROWS, PER)
    vmem = pl.BlockSpec(memory_space=pltpu.VMEM)
    hbm = pl.BlockSpec(memory_space=pl.ANY)
    dma = pltpu.SemaphoreType.DMA
    vg, d = pl.pallas_call(
        functools.partial(kernel, dims),
        out_shape=(
            jax.ShapeDtypeStruct((C, 2, SL, N), F32),
            jax.ShapeDtypeStruct((C, PER, ROWS, ATOMS), F32),
        ),
        in_specs=[hbm, vmem, pl.BlockSpec(memory_space=pltpu.SMEM), vmem, hbm],
        out_specs=(vmem, vmem),
        scratch_shapes=[
            pltpu.VMEM((H, C, ZC, YL, N), F32),
            pltpu.VMEM((PAIRS, SL, N), BF16),
            pltpu.VMEM((N // 128, ROWS * PER * SL, 128), F32),
            pltpu.VMEM((ROWS * PER, SL * N), BF16),
            pltpu.VMEM((3 * N, 2 * S), BF16),
            pltpu.VMEM((2, YL, S), F32),
            pltpu.VMEM((3 * N, 2 * N), BF16),
            pltpu.VMEM((2, C, ZC, S), F32),
            pltpu.VMEM((H, F, ZC, 2 * C * SL), F32),
            pltpu.VMEM((G, F, H, ZC, 2 * C * SL), F32),
            pltpu.VMEM((2, SL, ATOMS, N), F32),
            pltpu.VMEM((3, ATOMS, N), jnp.int32),
            pltpu.VMEM((ZC * YL, 2 * S), F32),
            pltpu.VMEM((ATOMS, SL * N), BF16),
            pltpu.VMEM((C, PER, ROWS, ATOMS), F32),
            pltpu.VMEM((F, ROWS, ATOMS), F32),
            pltpu.VMEM((ROWS, ATOMS), F32),
            dma((H, C)), dma, dma((H, ND)), dma((H, ND)), dma((H,)),
            dma((F,)), dma((F,)), dma((F,)), dma((F,)),
        ],
        compiler_params=pltpu.CompilerParams(
            collective_id=0, has_side_effects=True, vmem_limit_bytes=60 * 1024 * 1024),
    )(potential, stick_mill, stick_mill, positions, aug_charge)
    return vg, d.reshape(C, PER * ROWS, ATOMS)[:, :PAIRS]


def solution(mesh):
    placed = (P(None, "fft", "grp", None), P(), P(None, "grp"), P(None, "fft", None))
    return jax.shard_map(
        body,
        mesh=mesh,
        in_specs=placed,
        out_specs=(P(None, None, "fft", None), P(None, None, "grp")),
        check_vma=False,
    )
```

profile of v0, /device:TPU:24, one launch (start us, length us, event | category | flops | bytes accessed | tf_op | source)
XLA Modules:
  0.0 50.9 jit_solution(14578789562681543656)
XLA Ops:
  0.6 46.8 %shard_map.59 = (f32[4,2,16,256]{3,2,1,0:T(8,128)}, f32[4,4,48,128]{3,2,1,0:T(8,128)}) custom-call(f32[4,16,128,256]{3,2,1,0:T(8,128)} %pot_hbm.1, s32[2,256]{1,0:T(2,128)} %mill_smem.1, s32[2,256]{1,0:T(2,128)} %mill_smem.1, s32[3,128]{1,0:T(4,128)} %pos_ref.1, bf16[171,16,256]{2,1,0:T(8,128)(2,1)} %aug_hbm.1), custom_call_target="tpu_custom_call" | custom-call | tf_op jit(solution)/shard_map/pallas_call | solution.py:289
  47.4 1.0 %slice.4 = f32[4,171,128]{2,1,0:T(8,128)S(1)} slice(f32[4,192,128]{2,1,0:T(8,128)} %bitcast.1), slice={[0:4], [0:171], [0:128]} | slice | bytes 700416 | tf_op jit(solution)/shard_map/slice | solution.py:321
  48.4 0.9 %copy.7 = f32[4,171,128]{2,0,1:T(4,128)} copy(f32[4,171,128]{2,1,0:T(8,128)S(1)} %slice.4) | data formatting | bytes 700416
  49.3 1.6 %copy.9 = f32[4,2,16,256]{3,2,1,0:T(8,128)} copy(f32[4,2,16,256]{3,2,1,0:T(8,128)} %get-tuple-element.8) | data formatting | bytes 262144
where the time goes:
time: 51.3 us; the launch traced here: 50.9 us
  Pallas kernels  46.8 us (91%)
  local copies, waits for them, and re-layouts  3.45 us (7%)
  between operations  0.64 us (1%)
    pallas_call x1, Pallas kernels, body(): pl.pallas_call(functools.partial(kernel, dims), out_shape=(jax.ShapeDtype...  46.8 us
    unnamed x2, local copies, waits for them, and re-layouts  2.43 us

commit v1 on v0

--- a/solution.py
+++ b/solution.py
@@ -85,8 +85,6 @@
     ty[0] = cy
     ty[1] = sy
 
-    pl.semaphore_wait(barrier, ND - 1)
-
     def block_send(h, k):
         peer = lax.rem(me + k, ND)
         pf, pg = peer // G, lax.rem(peer, G)
@@ -103,8 +101,8 @@
             send_sem=s1.at[h, pf * G + pg], recv_sem=r1.at[h, peer],
             device_id={"fft": pf, "grp": pg}, device_id_type=MESH)
 
-    def group(h, _):
-        def component(c, _):
+    for h in range(H):
+        def component(c, _, h=h):
             pot_copy(h, c).wait()
             data = pot[h, c].reshape(ZC * YL, N)
             xmid[...] = jnp.dot(stack_data(data), tx[...], preferred_element_type=F32)
@@ -120,19 +118,18 @@
             return 0
 
         lax.fori_loop(0, C, component, 0)
+        if h == 0:
+            pl.semaphore_wait(barrier, ND - 1)
         for f in range(F):
             pieces = [part[ri, c, :, f * SL:(f + 1) * SL] for ri in range(2) for c in range(C)]
             send[h, f] = jnp.concatenate(pieces, axis=1)
 
-        def start(k, _):
+        def start(k, _, h=h):
             block_send(h, k).start()
             return 0
 
         lax.fori_loop(1, ND, start, 0)
         pltpu.make_async_copy(send.at[h, my_f], recv.at[my_g, my_f, h], own_sem.at[h]).start()
-        return 0
-
-    lax.fori_loop(0, H, group, 0)
 
     row = lax.broadcasted_iota(jnp.int32, (N, N), 0)
     col = lax.broadcasted_iota(jnp.int32, (N, N), 1) - N // 2

time: 51.3 us -> 47.9 us (0.934)
  Pallas kernels: 46.8 us -> 43.6 us
    pallas_call x1, Pallas kernels: 46.8 us -> 43.6 us  [body(): pl.pallas_call(functools.partial(kernel, dims), out_shape=(jax.ShapeDtype...]
where the time goes in v1:
time: 47.9 us; the launch traced here: 47.7 us
  Pallas kernels  43.6 us (91%)
  local copies, waits for them, and re-layouts  3.45 us (7%)
  between operations  0.64 us (1%)
    pallas_call x1, Pallas kernels, body(): pl.pallas_call(functools.partial(kernel, dims), out_shape=(jax.ShapeDtype...  43.6 us
    unnamed x2, local copies, waits for them, and re-layouts  2.43 us
    slice x1, local copies, waits for them, and re-layouts, body(): return (vg, d.reshape(C, PER * ROWS, ATOMS)[:, :PAIRS])  1.01 us

profile of v1, /device:TPU:24, one launch (start us, length us, event | category | flops | bytes accessed | tf_op | source)
XLA Modules:
  0.0 47.7 jit_solution(124910600423444102)
XLA Ops:
  0.6 43.6 %shard_map.59 = (f32[4,2,16,256]{3,2,1,0:T(8,128)}, f32[4,4,48,128]{3,2,1,0:T(8,128)}) custom-call(f32[4,16,128,256]{3,2,1,0:T(8,128)} %pot_hbm.1, s32[2,256]{1,0:T(2,128)} %mill_smem.1, s32[2,256]{1,0:T(2,128)} %mill_smem.1, s32[3,128]{1,0:T(4,128)} %pos_ref.1, bf16[171,16,256]{2,1,0:T(8,128)(2,1)} %aug_hbm.1), custom_call_target="tpu_custom_call" | custom-call | tf_op jit(solution)/shard_map/pallas_call | solution.py:286
  44.3 1.0 %slice.4 = f32[4,171,128]{2,1,0:T(8,128)S(1)} slice(f32[4,192,128]{2,1,0:T(8,128)} %bitcast.1), slice={[0:4], [0:171], [0:128]} | slice | bytes 700416 | tf_op jit(solution)/shard_map/slice | solution.py:318
  45.3 0.9 %copy.7 = f32[4,171,128]{2,0,1:T(4,128)} copy(f32[4,171,128]{2,1,0:T(8,128)S(1)} %slice.4) | data formatting | bytes 700416
  46.1 1.6 %copy.9 = f32[4,2,16,256]{3,2,1,0:T(8,128)} copy(f32[4,2,16,256]{3,2,1,0:T(8,128)} %get-tuple-element.8) | data formatting | bytes 262144

commit v2 on v1

--- a/solution.py
+++ b/solution.py
@@ -47,8 +47,8 @@
 
 
 def kernel(dims, pot_hbm, mill_ref, mill_smem, pos_ref, aug_hbm, vg_ref, d_ref,
-           pot, aug, augf, qall, tx, ty, tz, part, send, recv, phase, kpos, xmid, mixed, dpart, dbuf, dsum,
-           pot_sem, aug_sem, s1, r1, own_sem, s2, r2, s3, r3):
+           pot, aug, augf, qall, tx, ty, tz, part, send, recv, phase, kpos, xmid, mixed, dpart, dbuf, dsum, dfar,
+           pot_sem, aug_sem, s1, r1, own_sem, s2, r2, s3, r3, s4, r4, s5, r5):
     C, ZL, YL, N, S, F, G, SL, PAIRS, ATOMS, ZC, ROWS, PER = dims
     H = ZL // ZC
     ND = F * G
@@ -192,12 +192,33 @@
 
     my_c, my_j = my_f // PER, lax.rem(my_f, PER)
 
-    def d_send(ci, j):
-        owner = ci * PER + j
-        return pltpu.make_async_remote_copy(
-            src_ref=dpart.at[ci, j], dst_ref=dbuf.at[my_f],
-            send_sem=s2.at[owner], recv_sem=r2.at[my_f],
-            device_id={"fft": owner}, device_id_type=MESH)
+    def line_send(ci, k):
+        j = lax.rem(my_j + k, PER)
+        return pltpu.make_async_remote_copy(
+            src_ref=dpart.at[ci, j], dst_ref=dbuf.at[ci, my_j],
+            send_sem=s2.at[ci, j], recv_sem=r2.at[ci, my_j],
+            device_id={"fft": my_c * PER + j}, device_id_type=MESH)
+
+    def line_recv(ci, k):
+        j = lax.rem(my_j + k, PER)
+        return pltpu.make_async_remote_copy(
+            src_ref=dpart.at[ci, j], dst_ref=dbuf.at[ci, j],
+            send_sem=s2.at[ci, j], recv_sem=r2.at[ci, j],
+            device_id={"fft": my_c * PER + j}, device_id_type=MESH)
+
+    def far_copy(k, src, dst, slot, ssem, rsem):
+        ci = lax.rem(my_c + k, C)
+        return pltpu.make_async_remote_copy(
+            src_ref=src, dst_ref=dst, send_sem=ssem.at[ci], recv_sem=rsem.at[slot],
+            device_id={"fft": ci * PER + my_j}, device_id_type=MESH)
+
+    def near_copy(ci, k, mine):
+        j = lax.rem(my_j + k, PER)
+        slot = my_j if mine else j
+        return pltpu.make_async_remote_copy(
+            src_ref=d_ref.at[ci, slot], dst_ref=d_ref.at[ci, slot],
+            send_sem=s5.at[ci, j], recv_sem=r5.at[ci, slot],
+            device_id={"fft": my_c * PER + j}, device_id_type=MESH)
 
     def contract(i, _):
         ci = lax.rem(my_c + 1 + i, C)
@@ -208,43 +229,43 @@
         out = lax.dot_general(qall[...], mixed[...], (((1,), (1,)), ((), ())), preferred_element_type=F32)
         for j in range(PER):
             dpart[ci, j] = out[j * ROWS:(j + 1) * ROWS]
-        for j in range(PER):
-            @pl.when(ci * PER + j != my_f)
-            def _():
-                d_send(ci, j).start()
+        for k in range(1, PER):
+            line_send(ci, k).start()
         return 0
 
     lax.fori_loop(0, C, contract, 0)
 
-    dbuf[my_f] = dpart[my_c, my_j]
-
-    def d_wait(k, _):
-        peer = lax.rem(my_f + k, F)
-        pltpu.make_async_remote_copy(
-            src_ref=dpart.at[peer // PER, lax.rem(peer, PER)], dst_ref=dbuf.at[peer],
-            send_sem=s2.at[peer], recv_sem=r2.at[peer],
-            device_id={"fft": peer}, device_id_type=MESH).wait_recv()
-        return 0
-
-    lax.fori_loop(1, F, d_wait, 0)
-    total = dbuf[0]
-    for f in range(1, F):
-        total = total + dbuf[f]
-    dsum[...] = total
-
-    def out_copy(k):
-        peer = lax.rem(my_f + k, F)
-        return pltpu.make_async_remote_copy(
-            src_ref=dsum, dst_ref=d_ref.at[my_c, my_j],
-            send_sem=s3.at[peer], recv_sem=r3.at[my_f],
-            device_id={"fft": peer}, device_id_type=MESH)
-
-    def out_start(k, _):
-        out_copy(k).start()
-        return 0
-
-    lax.fori_loop(1, F, out_start, 0)
+    for i in range(C):
+        ci = lax.rem(my_c + 1 + i, C)
+        dbuf[ci, my_j] = dpart[ci, my_j]
+        for k in range(1, PER):
+            line_recv(ci, k).wait_recv()
+        part_sum = dbuf[ci, 0]
+        for j in range(1, PER):
+            part_sum = part_sum + dbuf[ci, j]
+        dsum[ci] = part_sum
+        if i < C - 1:
+            far_copy(i + 1, dsum.at[ci], dfar.at[my_c], my_c, s4, r4).start()
+        else:
+            dfar[my_c] = part_sum
+    for k in range(1, C):
+        ci = lax.rem(my_c + k, C)
+        far_copy(k, dsum.at[ci], dfar.at[ci], ci, s4, r4).wait_recv()
+    total = dfar[0]
+    for c in range(1, C):
+        total = total + dfar[c]
     d_ref[my_c, my_j] = total
+    here = d_ref.at[my_c, my_j]
+    for k in range(1, C):
+        far_copy(k, here, here, my_c, s3, r3).start()
+    for k in range(1, PER):
+        near_copy(my_c, k, True).start()
+    for k in range(1, C):
+        ci = lax.rem(my_c + k, C)
+        there = d_ref.at[ci, my_j]
+        far_copy(k, there, there, ci, s3, r3).wait_recv()
+        for n in range(1, PER):
+            near_copy(ci, n, True).start()
 
     def drain(k, _):
         for h in range(H):
@@ -253,18 +274,15 @@
 
     lax.fori_loop(1, ND, drain, 0)
 
-    def finish(k, _):
-        peer = lax.rem(my_f + k, F)
-        pf, pj = peer // PER, lax.rem(peer, PER)
-        d_send(pf, pj).wait_send()
-        out_copy(k).wait_send()
-        pltpu.make_async_remote_copy(
-            src_ref=dsum, dst_ref=d_ref.at[pf, pj],
-            send_sem=s3.at[peer], recv_sem=r3.at[peer],
-            device_id={"fft": peer}, device_id_type=MESH).wait_recv()
-        return 0
-
-    lax.fori_loop(1, F, finish, 0)
+    for i in range(C):
+        ci = lax.rem(my_c + i, C)
+        for k in range(1, PER):
+            line_send(ci, k).wait_send()
+            near_copy(ci, k, True).wait_send()
+            near_copy(ci, k, False).wait_recv()
+        if i > 0:
+            far_copy(i, dsum.at[ci], dfar.at[my_c], my_c, s4, r4).wait_send()
+            far_copy(i, here, here, my_c, s3, r3).wait_send()
 
 
 def body(potential, stick_mill, positions, aug_charge):
@@ -307,10 +325,12 @@
             pltpu.VMEM((ZC * YL, 2 * S), F32),
             pltpu.VMEM((ATOMS, SL * N), BF16),
             pltpu.VMEM((C, PER, ROWS, ATOMS), F32),
-            pltpu.VMEM((F, ROWS, ATOMS), F32),
-            pltpu.VMEM((ROWS, ATOMS), F32),
+            pltpu.VMEM((C, PER, ROWS, ATOMS), F32),
+            pltpu.VMEM((C, ROWS, ATOMS), F32),
+            pltpu.VMEM((C, ROWS, ATOMS), F32),
             dma((H, C)), dma, dma((H, ND)), dma((H, ND)), dma((H,)),
-            dma((F,)), dma((F,)), dma((F,)), dma((F,)),
+            dma((C, PER)), dma((C, PER)), dma((C,)), dma((C,)),
+            dma((C,)), dma((C,)), dma((C, PER)), dma((C, PER)),
         ],
         compiler_params=pltpu.CompilerParams(
             collective_id=0, has_side_effects=True, vmem_limit_bytes=60 * 1024 * 1024),

time: 47.9 us -> 46 us (0.960)
  the two profiles are of different devices: /device:TPU:24 before, /device:TPU:0 now
where the time goes in v2:
time: 46 us; the launch traced here: 45.8 us
  Pallas kernels  41.7 us (91%)
  local copies, waits for them, and re-layouts  3.45 us (8%)
  between operations  0.64 us (1%)
    pallas_call x1, Pallas kernels, body(): pl.pallas_call(functools.partial(kernel, dims), out_shape=(jax.ShapeDtype...  41.7 us
    unnamed x2, local copies, waits for them, and re-layouts  2.43 us
    slice x1, local copies, waits for them, and re-layouts, body(): return (vg, d.reshape(C, PER * ROWS, ATOMS)[:, :PAIRS])  1.01 us

profile of v2, /device:TPU:0, one launch (start us, length us, event | category | flops | bytes accessed | tf_op | source)
XLA Modules:
  0.0 45.8 jit_solution(1184425016725087125)
XLA Ops:
  0.6 41.7 %shard_map.59 = (f32[4,2,16,256]{3,2,1,0:T(8,128)}, f32[4,4,48,128]{3,2,1,0:T(8,128)}) custom-call(f32[4,16,128,256]{3,2,1,0:T(8,128)} %pot_hbm.1, s32[2,256]{1,0:T(2,128)} %mill_smem.1, s32[2,256]{1,0:T(2,128)} %mill_smem.1, s32[3,128]{1,0:T(4,128)} %pos_ref.1, bf16[171,16,256]{2,1,0:T(8,128)(2,1)} %aug_hbm.1), custom_call_target="tpu_custom_call" | custom-call | tf_op jit(solution)/shard_map/pallas_call | solution.py:304
  42.3 1.0 %slice.4 = f32[4,171,128]{2,1,0:T(8,128)S(1)} slice(f32[4,192,128]{2,1,0:T(8,128)} %bitcast.1), slice={[0:4], [0:171], [0:128]} | slice | bytes 700416 | tf_op jit(solution)/shard_map/slice | solution.py:338
  43.3 0.9 %copy.7 = f32[4,171,128]{2,0,1:T(4,128)} copy(f32[4,171,128]{2,1,0:T(8,128)S(1)} %slice.4) | data formatting | bytes 700416
  44.2 1.6 %copy.9 = f32[4,2,16,256]{3,2,1,0:T(8,128)} copy(f32[4,2,16,256]{3,2,1,0:T(8,128)} %get-tuple-element.8) | data formatting | bytes 262144
